TPU v7x, 256 devices: a whole 4x4x8 slice. The times are simulated.
256 devices in a mesh: ep: 32 (over z, y), tp: 8 (over x, core).
Axes of the slice: x: 4, y: 4, z: 8, core: 2. Of those that a mesh axis runs over, the one named last changes fastest.
Arguments:
- tokens: bfloat16 [4096, 2048], P('ep', 'tp'), may hold values from -200 to 200
- norm_gain: bfloat16 [2048], P('tp'), may hold values from 0.099609375 to 1.8984375
- router_logits: float32 [4096, 64], P('ep'), may hold values from -8 to 400
- routes: int32 [4096, 8], P('ep'), may hold values from 0 to 63, all different within a row; in each aligned block of 128 rows (0 to 127, 128 to 255, ...) at most 32 rows name the same one
- gate_proj: bfloat16 [64, 2048, 1024], P('ep', None, 'tp'), may hold values from -0.125 to 0.125
- up_proj: bfloat16 [64, 2048, 1024], P('ep', None, 'tp'), may hold values from -0.125 to 0.125
- down_proj: bfloat16 [64, 1024, 2048], P('ep', 'tp'), may hold values from -0.1875 to 0.1875
Outputs:
- mixed: bfloat16 [4096, 2048], P('ep', 'tp')
Inputs may be any that keep to these rules, and one draw needn't show every extreme that they name: `routes`: within each aligned block of 128 rows (the tokens of one index of ep) no expert is named by more than 32 rows, a bound that some block reaches; a row names 8 different experts.
All inputs are finite; a program needn't handle non-finite values.
Results may differ from a plain program's by a relative error of at most 0.0071.
Values may be sent and summed in bfloat16 or wider, within the bound.
No kernel may reach another device: no remote copies, remote signals or barrier semaphores. Data moves between devices by JAX's collectives and lax.ppermute only.
A program may use at most 128 MiB of HBM per device.

v0:
```python
import jax
import jax.numpy as jnp
from jax import lax
from jax.sharding import PartitionSpec as P

epsilon = 1e-05


def on_device(tokens, norm_gain, router_logits, routes, gate_proj, up_proj, down_proj):
    ep_count = lax.axis_size("ep")
    group_size = tokens.shape[0]
    width = tokens.shape[1]
    top_count = routes.shape[1]
    local_experts = gate_proj.shape[0]
    expert_count = local_experts * ep_count
    capacity = 2 * group_size * top_count // expert_count
    slot_count = expert_count * capacity
    expert_iota = jnp.arange(expert_count, dtype=jnp.int32)
    flat_routes = routes.reshape(-1)
    route_hits = (flat_routes[:, None] == expert_iota[None, :]).astype(jnp.int32)
    position = jnp.sum((jnp.cumsum(route_hits, axis=0) - route_hits) * route_hits, axis=1)
    slot_grid = (flat_routes * capacity + position).reshape(group_size, top_count)
    chosen = jnp.sum(
        jnp.where(routes[:, :, None] == expert_iota[None, None, :], router_logits[:, None, :], 0.0),
        axis=-1,
    )
    gates = jax.nn.softmax(chosen, axis=-1)
    matches = jnp.arange(slot_count, dtype=jnp.int32)[:, None, None] == slot_grid[None, :, :]
    dispatch_table = jnp.any(matches, axis=-1).astype(jnp.bfloat16)
    whole, gain_all = (
        lax.all_gather(tokens, "tp", axis=1, tiled=True),
        lax.all_gather(norm_gain, "tp", axis=0, tiled=True),
    )
    floated = whole.astype(jnp.float32)
    mean_square = jnp.mean(floated * floated, axis=-1, keepdims=True)
    normed = (floated * lax.rsqrt(mean_square + epsilon) * gain_all.astype(jnp.float32)).astype(
        jnp.bfloat16
    )
    outgoing = jnp.dot(dispatch_table, normed, preferred_element_type=jnp.float32).astype(
        jnp.bfloat16
    )
    arrived = lax.all_to_all(outgoing, "ep", split_axis=0, concat_axis=0, tiled=True)
    arrived = arrived.reshape(ep_count, local_experts, capacity, arrived.shape[1])
    gate_val = jnp.einsum("slcd,ldh->slch", arrived, gate_proj, preferred_element_type=jnp.float32)
    up_val = jnp.einsum("slcd,ldh->slch", arrived, up_proj, preferred_element_type=jnp.float32)
    hidden = (jax.nn.silu(gate_val) * up_val).astype(jnp.bfloat16)
    term = jnp.einsum("slch,lhd->dslc", hidden, down_proj, preferred_element_type=jnp.float32)
    summed = lax.psum_scatter(
        term.reshape(width * lax.axis_size("tp"), slot_count), "tp", scatter_dimension=0, tiled=True
    )
    returned = lax.all_to_all(
        summed.astype(jnp.bfloat16), "ep", split_axis=1, concat_axis=1, tiled=True
    )
    slot_rows = jnp.transpose(returned)
    picked = slot_rows[slot_grid].astype(jnp.float32)
    mixed = jnp.sum(gates[:, :, None] * picked, axis=1)
    return mixed.astype(jnp.bfloat16)


def solution(mesh):
    return jax.shard_map(
        on_device,
        mesh=mesh,
        in_specs=(
            P("ep", "tp"),
            P("tp"),
            P("ep", None),
            P("ep", None),
            P("ep", None, "tp"),
            P("ep", None, "tp"),
            P("ep", "tp", None),
        ),
        out_specs=P("ep", "tp"),
        check_vma=False,
    )
```

profile of v0, /device:TPU:8, one launch (start us, length us, event | category | flops | bytes accessed | tf_op | source)
XLA Modules:
  0.0 431.7 jit_solution(2664050021449953185)
XLA Ops:
  6.5 0.0 copy-start
  6.5 0.0 reduce-scatter.2.cloned.1.call-start
  6.5 0.9 copy.44
  7.4 0.1 eq.59
  7.5 0.1 eq.55
  7.6 18.0 %reduce-window.6 = s32[64,8,128]{2,1,0:T(8,128)S(1)} reduce-window(s32[64,8,128]{2,1,0:T(8,128)S(1)} %fusion.39, s32[]{:T(128)} %constant.12.clone.1), window={size=1x1x128 pad=0_0x0_0x127_0}, to_apply=%region_3.4 | reduce-window | flops 8323072 | bytes 524292 | tf_op jit(solution)/shard_map/reduce-window
  25.6 0.1 slice.10
  25.8 0.1 copy.46
  26.0 0.1 copy.47
  26.0 0.1 broadcast_add_fusion
  26.2 0.1 fusion.38
  26.3 0.1 reduce_sum.50
  26.4 0.7 compare_select_fusion
  27.1 7.4 %fusion = pred[2048,128]{1,0:T(8,128)(4,1)S(1)} fusion(s32[128,8]{0,1:T(8,128)S(1)} %get-tuple-element.6), kind=kLoop, calls=%fused_computation.2 | loop fusion | flops 3932160 | bytes 266240 | tf_op jit(solution)/shard_map/reduce_or | solution.py:29
  34.5 13.7 %all_gather.6 = bf16[128,2048]{1,0:T(8,128)(2,1)S(1)} all-gather(bf16[128,256]{1,0:T(8,128)(2,1)} %param.7), channel_id=1, replica_groups=mesh['ep'=32,'tp'=8] {'tp'}, dimensions={1}, use_global_device_ids=true | all-gather | bytes 589824 | tf_op jit(solution)/shard_map/all_gather | solution.py:31
  48.2 0.2 fusion.19
  48.4 0.7 reshape.97
  49.1 10.2 %all-gather = bf16[8,1,256]{2,1,0:T(2,128)(2,1)S(1)} all-gather(bf16[1,1,256]{2,1,0:T(2,128)(2,1)S(1)} %reshape.97), channel_id=1, replica_groups=mesh['ep'=32,'tp'=8] {'tp'}, dimensions={0}, use_global_device_ids=true | all-gather | bytes 4608 | tf_op jit(solution)/shard_map/all_gather | solution.py:32
  59.3 2.4 convolution_convert_fusion
  61.7 0.0 copy-start.5
  61.7 197.5 %all_to_all.21 = bf16[32,64,2048]{2,1,0:T(8,128)(2,1)S(1)} all-to-all(bf16[32,64,2048]{2,1,0:T(8,128)(2,1)S(1)} %bitcast.59), channel_id=1, replica_groups=mesh['ep'=32,'tp'=8] {'ep'}, dimensions={0} | all-to-all | bytes 16777216 | tf_op jit(solution)/shard_map/all_to_all | solution.py:42
  259.2 0.0 copy-start.1
  259.2 0.0 copy-start.2
  259.2 3.2 copy-done.1
  262.4 0.0 copy-done.5
  262.4 2.3 fusion.5
  264.7 0.0 copy-done
  264.7 0.0 copy-done.2
  264.7 14.1 %convolution_bitcast_fusion = f32[2048,32,2,32]{0,3,1,2:T(8,128)} fusion(bf16[32,2,32,2048]{3,2,1,0:T(8,128)(2,1)} %bitcast.61, bf16[2,128,2048]{2,1,0:T(8,128)(2,1)S(1)} %copy-done, bf16[2,2048,128]{2,1,0:T(8,128)(2,1)S(1)} %copy-done.2, f32[32,2,32,128]{3,2,0,1:T(8,128)S(1)} %fusion.5), kind=kOutput, calls=%fused_computation.8 | convolution fusion | flops 2149056512 | bytes 28311552 | tf_op jit(solution)/shard_map/slch,lhd->dslc/dot_general | solution.py:47
  278.9 11.6 %copy.51 = f32[2048,32,2,32]{0,3,2,1:T(8,128)} copy(f32[2048,32,2,32]{0,3,1,2:T(8,128)} %convolution_bitcast_fusion) | data formatting | bytes 33554432 | tf_op jit(solution)/shard_map/slch,lhd->dslc/transpose | solution.py:47
  290.5 0.0 copy-start.3
  290.5 0.0 copy-start.4
  290.5 0.0 reduce-scatter.2.cloned.1.call-update
  290.5 89.0 %reduce-scatter.2.cloned.1.call-done = f32[256,2048]{0,1:T(8,128)} async-done(((f32[2048,2048]{0,1:T(8,128)}), f32[256,2048]{0,1:T(8,128)}) %reduce-scatter.2.cloned.1.call-update) | async-done | bytes 2097168 | tf_op jit(solution)/shard_map/reduce_scatter | solution.py:48
  379.5 2.7 convert_element_type.39
  382.2 10.2 %all-to-all-start.1 = ((bf16[256,32,64]{0,2,1:T(8,128)(2,1)}), bf16[256,32,64]{0,2,1:T(8,128)(2,1)S(1)}, u32[]{:S(2)}, u32[]{:S(2)}) async-start(bf16[256,32,64]{0,2,1:T(8,128)(2,1)} %bitcast.15), calls=%async_computation.2 | async-start | bytes 2097152 | tf_op jit(solution)/shard_map/all_to_all | solution.py:51
  392.4 0.1 copy.52
  392.5 0.1 reshape.88
  392.5 0.0 copy-done.3
  392.6 0.0 copy-done.4
  392.7 0.1 copy.43
  392.8 27.1 %all-to-all-done.1 = bf16[256,32,64]{0,2,1:T(8,128)(2,1)S(1)} async-done(((bf16[256,32,64]{0,2,1:T(8,128)(2,1)}), bf16[256,32,64]{0,2,1:T(8,128)(2,1)S(1)}, u32[]{:S(2)}, u32[]{:S(2)}) %all-to-all-start.1) | async-done | bytes 1048608 | tf_op jit(solution)/shard_map/all_to_all | solution.py:51
  419.9 3.9 gather_fusion
  423.8 1.0 fusion.22
  (11 shorter events, 0.2 us)
Async XLA Ops:
  6.5 258.2 %copy-start = (bf16[2,128,2048]{2,1,0:T(8,128)(2,1)S(1)}, bf16[2,128,2048]{2,1,0:T(8,128)(2,1)}, u32[]{:S(2)}) copy-start(bf16[2,128,2048]{2,1,0:T(8,128)(2,1)} %param.13) | copy-start | bytes 3145732
  6.5 373.0 %reduce-scatter.2.cloned.1.call-start = ((), (), s32[]{:S(2)}) async-start(), calls=%async_computation.3 | async-start | bytes 18874368 | tf_op jit(solution)/shard_map/reduce_scatter | solution.py:48
  61.7 200.7 %copy-start.5 = (bf16[2,2048,128]{2,1,0:T(8,128)(2,1)S(1)}, bf16[2,2048,128]{2,1,0:T(8,128)(2,1)}, u32[]{:S(2)}) copy-start(bf16[2,2048,128]{2,1,0:T(8,128)(2,1)} %param.11) | copy-start | bytes 3145732
  259.2 3.2 copy-start.1
  259.2 5.6 %copy-start.2 = (bf16[2,2048,128]{2,1,0:T(8,128)(2,1)S(1)}, bf16[2,2048,128]{2,1,0:T(8,128)(2,1)}, u32[]{:S(2)}) copy-start(bf16[2,2048,128]{2,1,0:T(8,128)(2,1)} %param.12) | copy-start | bytes 3145732
  290.5 102.1 %copy-start.3 = (s32[128,8]{0,1:T(8,128)S(1)}, s32[128,8]{0,1:T(8,128)}, u32[]{:S(2)}) copy-start(s32[128,8]{0,1:T(8,128)} %param.10) | copy-start | bytes 12292
  290.5 102.1 %copy-start.4 = (f32[128,64]{0,1:T(8,128)S(1)}, f32[128,64]{0,1:T(8,128)}, u32[]{:S(2)}) copy-start(f32[128,64]{0,1:T(8,128)} %param.9) | copy-start | bytes 98308
  382.2 37.7 %all-to-all-start.1 = ((bf16[256,32,64]{0,2,1:T(8,128)(2,1)}), bf16[256,32,64]{0,2,1:T(8,128)(2,1)S(1)}, u32[]{:S(2)}, u32[]{:S(2)}) async-start(bf16[256,32,64]{0,2,1:T(8,128)(2,1)} %bitcast.15), calls=%async_computation.2 | async-start | bytes 2097152 | tf_op jit(solution)/shard_map/all_to_all | solution.py:51
Sparse Core Ops, SparseCore 0:
  290.6 88.8 reduce-scatter.1
where the time goes:
time: 432 us
  blocking collectives  221 us (51%)
  waiting for transfers between devices  116 us (27%)
  other arithmetic  30.4 us (7%)
  local copies, waits for them, and re-layouts  21.3 us (5%)
  matrix products  18.8 us (4%)
  between operations  13.6 us (3%)
  starting transfers between devices  10.2 us (2%)
    all_to_all x1, blocking collectives, on_device(): lax.all_to_all(outgoing, 'ep', split_axis=0, concat_axis=0, tiled=True)  197 us
    reduce_scatter x1, waiting for transfers between devices, on_device(): lax.psum_scatter(term.reshape(width * lax.axis_size('tp'), slot_count), '...  89 us
    all_to_all x1, waiting for transfers between devices, on_device(): lax.all_to_all(summed.astype(jnp.bfloat16), 'ep', split_axis=1, concat_ax...  27.1 us
    another operation x3, other arithmetic  18.2 us
    dot_general x1, matrix products, on_device(): jnp.einsum('slch,lhd->dslc', hidden, down_proj, preferred_element_type=jn...  14.1 us
    all_gather x1, blocking collectives, on_device(): lax.all_gather(tokens, 'tp', axis=1, tiled=True)  13.7 us
    transpose x1, local copies, waits for them, and re-layouts, on_device(): jnp.einsum('slch,lhd->dslc', hidden, down_proj, preferred_element_type=jn...  11.6 us
    all_gather x1, blocking collectives, on_device(): lax.all_gather(norm_gain, 'tp', axis=0, tiled=True)  10.2 us
  transfers between devices with their start and end apart: 2, of which 2 were waited for; matrix products, arithmetic and copies ran while one was open for 0% of the time, Pallas kernels for 0%

commit v1 on v0

--- a/solution.py
+++ b/solution.py
@@ -2,6 +2,7 @@
 import jax.numpy as jnp
 from jax import lax
 from jax.sharding import PartitionSpec as P
+from jax.lax import all_to_all, axis_size
 
 epsilon = 1e-05
 
@@ -48,8 +49,11 @@
     summed = lax.psum_scatter(
         term.reshape(width * lax.axis_size("tp"), slot_count), "tp", scatter_dimension=0, tiled=True
     )
-    returned = lax.all_to_all(
-        summed.astype(jnp.bfloat16), "ep", split_axis=1, concat_axis=1, tiled=True
+    returned = jnp.concatenate(
+        all_to_all(
+            jnp.stack(jnp.split(summed.astype(jnp.bfloat16), axis_size("ep"), axis=1)), "ep", 0, 0
+        ),
+        axis=1,
     )
     slot_rows = jnp.transpose(returned)
     picked = slot_rows[slot_grid].astype(jnp.float32)

time: 432 us -> 450 us (1.042)
  local copies, waits for them, and re-layouts: 21.3 us -> 40.7 us
    unnamed x14 -> x45, local copies, waits for them, and re-layouts: 4.78 us -> 23.5 us
where the time goes in v1:
time: 450 us
  blocking collectives  221 us (49%)
  waiting for transfers between devices  116 us (26%)
  local copies, waits for them, and re-layouts  40.7 us (9%)
  other arithmetic  29.4 us (7%)
  matrix products  18.8 us (4%)
  between operations  13.6 us (3%)
  starting transfers between devices  10.2 us (2%)
    all_to_all x1, blocking collectives, on_device(): lax.all_to_all(outgoing, 'ep', split_axis=0, concat_axis=0, tiled=True)  197 us
    reduce_scatter x1, waiting for transfers between devices, on_device(): lax.psum_scatter(term.reshape(width * lax.axis_size('tp'), slot_count), '...  89 us
    all_to_all x1, waiting for transfers between devices, on_device(): all_to_all(jnp.stack(jnp.split(summed.astype(jnp.bfloat16), axis_size('ep...  27.1 us
    unnamed x45, local copies, waits for them, and re-layouts  23.5 us
    another operation x3, other arithmetic  18.2 us
    dot_general x1, matrix products, on_device(): jnp.einsum('slch,lhd->dslc', hidden, down_proj, preferred_element_type=jn...  14.1 us
    all_gather x1, blocking collectives, on_device(): lax.all_gather(tokens, 'tp', axis=1, tiled=True)  13.7 us
    transpose x1, local copies, waits for them, and re-layouts, on_device(): jnp.einsum('slch,lhd->dslc', hidden, down_proj, preferred_element_type=jn...  11.6 us
  transfers between devices with their start and end apart: 2, of which 2 were waited for; matrix products, arithmetic and copies ran while one was open for 0% of the time, Pallas kernels for 0%

profile of v1, /device:TPU:8, one launch (start us, length us, event | category | flops | bytes accessed | tf_op | source)
XLA Modules:
  0.0 450.1 jit_solution(8107725817888526657)
XLA Ops:
  6.5 0.9 copy.44
  7.4 0.1 eq.59
  7.5 0.1 eq.55
  7.6 18.0 %reduce-window.6 = s32[64,8,128]{2,1,0:T(8,128)S(1)} reduce-window(s32[64,8,128]{2,1,0:T(8,128)S(1)} %fusion.39, s32[]{:T(128)} %constant.12.clone.1), window={size=1x1x128 pad=0_0x0_0x127_0}, to_apply=%region_3.4 | reduce-window | flops 8323072 | bytes 524292 | tf_op jit(solution)/shard_map/reduce-window
  25.6 0.1 slice.10
  25.8 0.1 copy.46
  26.0 0.1 copy.47
  26.0 0.1 broadcast_add_fusion
  26.2 0.1 fusion.38
  26.3 0.1 reduce_sum.50
  26.4 0.7 compare_select_fusion
  27.1 7.4 %fusion = pred[2048,128]{1,0:T(8,128)(4,1)S(1)} fusion(s32[128,8]{0,1:T(8,128)S(1)} %get-tuple-element.6), kind=kLoop, calls=%fused_computation.2 | loop fusion | flops 3932160 | bytes 266240 | tf_op jit(solution)/shard_map/reduce_or | solution.py:30
  34.5 13.7 %all_gather.6 = bf16[128,2048]{1,0:T(8,128)(2,1)S(1)} all-gather(bf16[128,256]{1,0:T(8,128)(2,1)} %param.7), channel_id=1, replica_groups=mesh['ep'=32,'tp'=8] {'tp'}, dimensions={1}, use_global_device_ids=true | all-gather | bytes 589824 | tf_op jit(solution)/shard_map/all_gather | solution.py:32
  48.2 0.2 fusion.19
  48.4 0.7 reshape.103
  49.1 10.2 %all-gather = bf16[8,1,256]{2,1,0:T(2,128)(2,1)S(1)} all-gather(bf16[1,1,256]{2,1,0:T(2,128)(2,1)S(1)} %reshape.103), channel_id=1, replica_groups=mesh['ep'=32,'tp'=8] {'tp'}, dimensions={0}, use_global_device_ids=true | all-gather | bytes 4608 | tf_op jit(solution)/shard_map/all_gather | solution.py:33
  59.3 2.4 convolution_convert_fusion
  61.7 197.5 %all_to_all.14 = bf16[32,64,2048]{2,1,0:T(8,128)(2,1)S(1)} all-to-all(bf16[32,64,2048]{2,1,0:T(8,128)(2,1)S(1)} %bitcast.188), channel_id=1, replica_groups=mesh['ep'=32,'tp'=8] {'ep'}, dimensions={0} | all-to-all | bytes 16777216 | tf_op jit(solution)/shard_map/all_to_all | solution.py:43
  259.2 3.2 copy-done.1
  262.4 2.3 fusion.5
  264.7 14.1 %convolution_bitcast_fusion = f32[2048,32,2,32]{0,3,1,2:T(8,128)} fusion(bf16[32,2,32,2048]{3,2,1,0:T(8,128)(2,1)} %bitcast.190, bf16[2,128,2048]{2,1,0:T(8,128)(2,1)S(1)} %copy-done, bf16[2,2048,128]{2,1,0:T(8,128)(2,1)S(1)} %copy-done.2, f32[32,2,32,128]{3,2,0,1:T(8,128)S(1)} %fusion.5), kind=kOutput, calls=%fused_computation.8 | convolution fusion | flops 2149056512 | bytes 28311552 | tf_op jit(solution)/shard_map/slch,lhd->dslc/dot_general | solution.py:48
  278.9 11.6 %copy.51 = f32[2048,32,2,32]{0,3,2,1:T(8,128)} copy(f32[2048,32,2,32]{0,3,1,2:T(8,128)} %convolution_bitcast_fusion) | data formatting | bytes 33554432 | tf_op jit(solution)/shard_map/slch,lhd->dslc/transpose | solution.py:48
  290.5 0.0 reduce-scatter.2.cloned.1.call-update
  290.5 89.0 %reduce-scatter.2.cloned.1.call-done = f32[256,2048]{0,1:T(8,128)} async-done(((f32[2048,2048]{0,1:T(8,128)}), f32[256,2048]{0,1:T(8,128)}) %reduce-scatter.2.cloned.1.call-update) | async-done | bytes 2097168 | tf_op jit(solution)/shard_map/reduce_scatter | solution.py:49
  379.5 1.7 convert_element_type.39
  381.2 0.6 constant_dynamic-update-slice_fusion.31
  381.8 0.6 constant_dynamic-update-slice_fusion.30
  382.4 0.6 constant_dynamic-update-slice_fusion.29
  383.0 0.6 constant_dynamic-update-slice_fusion.28
  383.6 0.6 constant_dynamic-update-slice_fusion.27
  384.2 0.6 constant_dynamic-update-slice_fusion.26
  384.8 0.6 constant_dynamic-update-slice_fusion.25
  385.4 0.6 constant_dynamic-update-slice_fusion.24
  386.1 0.6 constant_dynamic-update-slice_fusion.23
  386.7 0.6 constant_dynamic-update-slice_fusion.22
  387.3 0.6 constant_dynamic-update-slice_fusion.21
  387.9 0.6 constant_dynamic-update-slice_fusion.20
  388.5 0.6 constant_dynamic-update-slice_fusion.19
  389.1 0.6 constant_dynamic-update-slice_fusion.18
  389.7 0.6 constant_dynamic-update-slice_fusion.17
  390.3 0.6 constant_dynamic-update-slice_fusion.16
  390.9 0.6 constant_dynamic-update-slice_fusion.15
  391.5 0.6 constant_dynamic-update-slice_fusion.14
  392.1 0.6 constant_dynamic-update-slice_fusion.13
  392.7 0.6 constant_dynamic-update-slice_fusion.12
  393.3 0.6 constant_dynamic-update-slice_fusion.11
  393.9 0.6 constant_dynamic-update-slice_fusion.10
  394.5 0.6 constant_dynamic-update-slice_fusion.9
  395.1 0.6 constant_dynamic-update-slice_fusion.8
  395.7 0.6 constant_dynamic-update-slice_fusion.7
  396.3 0.6 constant_dynamic-update-slice_fusion.6
  396.9 0.6 constant_dynamic-update-slice_fusion.5
  397.5 0.6 constant_dynamic-update-slice_fusion.4
  398.1 0.6 constant_dynamic-update-slice_fusion.3
  398.7 0.6 constant_dynamic-update-slice_fusion.2
  399.4 0.6 constant_dynamic-update-slice_fusion.1
  400.0 0.6 constant_dynamic-update-slice_fusion
  400.6 10.2 %all-to-all-start.1 = ((bf16[32,256,64]{1,2,0:T(8,128)(2,1)}), bf16[32,256,64]{1,2,0:T(8,128)(2,1)S(1)}, u32[]{:S(2)}, u32[]{:S(2)}) async-start(bf16[32,256,64]{1,2,0:T(8,128)(2,1)} %constant_dynamic-update-slice_fusion), calls=%async_computation.2 | async-start | bytes 2097152 | tf_op jit(solution)/shard_map/all_to_all | solution.py:53
  410.7 0.1 copy.52
  410.8 0.1 reshape.94
  411.1 0.1 copy.43
  411.2 27.1 %all-to-all-done.1 = bf16[32,256,64]{1,2,0:T(8,128)(2,1)S(1)} async-done(((bf16[32,256,64]{1,2,0:T(8,128)(2,1)}), bf16[32,256,64]{1,2,0:T(8,128)(2,1)S(1)}, u32[]{:S(2)}, u32[]{:S(2)}) %all-to-all-start.1) | async-done | bytes 1048608 | tf_op jit(solution)/shard_map/all_to_all | solution.py:53
  438.3 3.9 gather_fusion
  442.2 1.0 fusion.22
  (23 shorter events, 0.2 us)
Async XLA Ops:
  6.5 258.2 %copy-start = (bf16[2,128,2048]{2,1,0:T(8,128)(2,1)S(1)}, bf16[2,128,2048]{2,1,0:T(8,128)(2,1)}, u32[]{:S(2)}) copy-start(bf16[2,128,2048]{2,1,0:T(8,128)(2,1)} %param.13) | copy-start | bytes 3145732
  6.5 373.0 %reduce-scatter.2.cloned.1.call-start = ((), (), s32[]{:S(2)}) async-start(), calls=%async_computation.3 | async-start | bytes 18874368 | tf_op jit(solution)/shard_map/reduce_scatter | solution.py:49
  61.7 200.7 %copy-start.5 = (bf16[2,2048,128]{2,1,0:T(8,128)(2,1)S(1)}, bf16[2,2048,128]{2,1,0:T(8,128)(2,1)}, u32[]{:S(2)}) copy-start(bf16[2,2048,128]{2,1,0:T(8,128)(2,1)} %param.11) | copy-start | bytes 3145732
  259.2 3.2 copy-start.1
  259.2 5.6 %copy-start.2 = (bf16[2,2048,128]{2,1,0:T(8,128)(2,1)S(1)}, bf16[2,2048,128]{2,1,0:T(8,128)(2,1)}, u32[]{:S(2)}) copy-start(bf16[2,2048,128]{2,1,0:T(8,128)(2,1)} %param.12) | copy-start | bytes 3145732
  290.5 120.4 %copy-start.3 = (s32[128,8]{0,1:T(8,128)S(1)}, s32[128,8]{0,1:T(8,128)}, u32[]{:S(2)}) copy-start(s32[128,8]{0,1:T(8,128)} %param.10) | copy-start | bytes 12292
  290.5 120.5 %copy-start.4 = (f32[128,64]{0,1:T(8,128)S(1)}, f32[128,64]{0,1:T(8,128)}, u32[]{:S(2)}) copy-start(f32[128,64]{0,1:T(8,128)} %param.9) | copy-start | bytes 98308
  400.6 37.7 %all-to-all-start.1 = ((bf16[32,256,64]{1,2,0:T(8,128)(2,1)}), bf16[32,256,64]{1,2,0:T(8,128)(2,1)S(1)}, u32[]{:S(2)}, u32[]{:S(2)}) async-start(bf16[32,256,64]{1,2,0:T(8,128)(2,1)} %constant_dynamic-update-slice_fusion), calls=%async_computation.2 | async-start | bytes 2097152 | tf_op jit(solution)/shard_map/all_to_all | solution.py:53
Sparse Core Ops, SparseCore 0:
  290.6 88.8 reduce-scatter.1
